TPU v7x, 32 devices: a whole 2x2x4 slice. The times are simulated.
32 devices in a mesh: tok: 8 (over z, y), voc: 4 (over x, core).
Axes of the slice: x: 2, y: 2, z: 4, core: 2. Of those that a mesh axis runs over, the one named last changes fastest.
Arguments:
- teacher_rows: bfloat16 [2048, 2048], P('tok', 'voc')
- drafter_rows: bfloat16 [2048, 2048], P('tok', 'voc')
- head: bfloat16 [2048, 16384], P(None, 'voc'), may hold values from -1 to 1
- fr_ids: int32 [16384], P('voc'), may hold values from 0 to 151935, as said below
- targets: int32 [2048], P('tok'), may hold values from 0 to 151935
- dest_index: int32 [2048], P('tok'), may hold values from -1 to 2047, as said below
- counts: int32 [8], replicated, may hold values from 64 to 256, as said below
Outputs:
- row_loss: float32 [2048], P('tok')
- drafter_grad: bfloat16 [2048, 2048], P('tok', 'voc')
Inputs may be any that keep to these rules, and one draw needn't show every extreme that they name: `dest_index`: the prefill rows that name a slot name distinct slots. With blocks of 256 rows and 8 blocks, a row of prefill block b names a slot of drafter block (b + k) mod 8 for k in 0, 1, 4, 5; at most 64 rows go from one prefill block to one drafter block, and every drafter block receives exactly 64 from its own prefill block. The slots named in drafter block j are exactly its first counts[j] slots, grouped by k in that order. counts[j] is the number of prefill rows that name a slot of block j; some block is full. `fr_ids`: distinct ids.
All inputs are finite; a program needn't handle non-finite values.
Results may differ from a plain program's by a relative error of at most 0.0041.
Values may be sent and summed in bfloat16 or wider, within the bound.
No kernel may reach another device: no remote copies, remote signals or barrier semaphores. Data moves between devices by JAX's collectives and lax.ppermute only.
A program may use at most 64 MiB of HBM per device.

v0:
```python
import jax
import jax.numpy as jnp
from jax import lax
from jax.sharding import PartitionSpec as P

REACH = 4


loss_scale = 16.0


def shifted(block, axis, distance):
    devices = range(lax.axis_size(axis))
    route = [((i - distance) % len(devices), i) for i in devices]
    return lax.ppermute(block, axis, route)


def encode(values):
    return jnp.stack([values // 128, values % 128], axis=1).astype(jnp.float32).astype(jnp.bfloat16)


def decode(code):
    widened = code.astype(jnp.float32)
    return (widened[:, 0] * 128.0 + widened[:, 1]).astype(jnp.int32)


def per_device(teacher_rows, drafter_rows, head, fr_ids, targets, dest_index, counts):
    row_count = teacher_rows.shape[0]
    tok_index = lax.axis_index("tok")
    slot_ids = jnp.arange(row_count, dtype=jnp.int32)
    tok_size = lax.axis_size("tok")
    capacity = row_count // REACH
    used = dest_index >= 0
    dest_owner = jnp.where(used, dest_index // row_count, 0)
    distance = (dest_owner - tok_index) % tok_size
    earlier = (
        (dest_owner[:, None] == dest_owner[None, :])
        & (dest_index[None, :] < dest_index[:, None])
        & used[None, :]
    )
    rank_in = jnp.sum(earlier.astype(jnp.int32), axis=1)
    local_dest = dest_index - dest_owner * row_count + 1
    cap_ids = jnp.arange(capacity, dtype=jnp.int32)
    buffers = []
    codes = []
    for offset in [0, 1, tok_size // 2, tok_size // 2 + 1]:
        select = (used & (distance == offset))[None, :] & (rank_in[None, :] == cap_ids[:, None])
        packed = jnp.dot(
            select.astype(jnp.bfloat16), teacher_rows, preferred_element_type=jnp.float32
        ).astype(jnp.bfloat16)
        packed_code = encode(jnp.sum(jnp.where(select, local_dest[None, :], 0), axis=1))
        if offset > 0:
            packed, packed_code = shifted((packed, packed_code), "tok", offset)
        buffers.append(packed)
        codes.append(packed_code)
    all_rows = jnp.concatenate(buffers, axis=0)
    arrived = decode(jnp.concatenate(codes, axis=0)) - 1
    select = (slot_ids[:, None] == arrived[None, :]).astype(jnp.bfloat16)
    moved = jnp.dot(select, all_rows, preferred_element_type=jnp.float32).astype(jnp.bfloat16)
    teacher_full, drafter_full = (
        lax.all_gather(moved, "voc", axis=1, tiled=True),
        lax.all_gather(drafter_rows, "voc", axis=1, tiled=True),
    )
    teach_logit = jnp.dot(teacher_full, head, preferred_element_type=jnp.float32)
    draft_logit = jnp.dot(drafter_full, head, preferred_element_type=jnp.float32)
    hit_table = (targets[:, None] == fr_ids[None, :]).astype(jnp.float32)
    local_hits = jnp.sum(hit_table, axis=1)
    local_target = jnp.sum(hit_table * draft_logit, axis=1)
    teach_max, draft_max = lax.pmax(
        (jnp.max(teach_logit, axis=1), jnp.max(draft_logit, axis=1)), "voc"
    )
    teach_exp = jnp.exp(teach_logit - teach_max[:, None])
    draft_exp = jnp.exp(draft_logit - draft_max[:, None])
    teach_total, draft_total, cross, target_logit, hits = lax.psum(
        (
            jnp.sum(teach_exp, axis=1),
            jnp.sum(draft_exp, axis=1),
            jnp.sum(teach_exp * (teach_logit - draft_logit), axis=1),
            local_target,
            local_hits,
        ),
        "voc",
    )
    valid = (slot_ids < counts[tok_index]).astype(jnp.float32)
    teach_lse = teach_max + jnp.log(teach_total)
    draft_lse = draft_max + jnp.log(draft_total)
    row_loss = valid * (
        cross / teach_total - teach_lse + draft_lse + hits * (draft_lse - target_logit)
    )
    teach_prob = teach_exp / teach_total[:, None]
    draft_prob = draft_exp / draft_total[:, None]
    grad_logit = (
        valid[:, None] * ((1.0 + hits)[:, None] * draft_prob - teach_prob - hit_table)
    ).astype(jnp.bfloat16)
    summed = lax.psum_scatter(
        lax.dot_general(
            head, grad_logit, (((1,), (1,)), ((), ())), preferred_element_type=jnp.float32
        ),
        "voc",
        scatter_dimension=0,
        tiled=True,
    )
    drafter_grad = (loss_scale * summed).T.astype(jnp.bfloat16)
    return (row_loss, drafter_grad)


def solution(mesh):
    return jax.shard_map(
        per_device,
        mesh=mesh,
        in_specs=(
            P("tok", "voc"),
            P("tok", "voc"),
            P(None, "voc"),
            P("voc"),
            P("tok"),
            P("tok"),
            P(),
        ),
        out_specs=(P("tok"), P("tok", "voc")),
        check_vma=False,
    )
```

profile of v0, /device:TPU:0, one launch (start us, length us, event | category | flops | bytes accessed | tf_op | source)
XLA Modules:
  0.0 135.4 jit_solution(9037898718361944399)
XLA Ops:
  7.2 0.0 copy-start
  7.2 0.0 all-gather.5.cloned.1.call-start
  7.2 0.7 all-gather.5.cloned.1.call-update
  7.9 0.0 all-gather.3.cloned.1.call-start
  8.0 0.7 subtract_add_fusion
  8.7 1.0 convert_reduce_fusion.1
  9.7 0.2 select_reduce_fusion.3
  9.9 4.1 %collective-permute-start.1 = (bf16[64,2]{0,1:T(2,128)(2,1)S(1)}, bf16[64,2]{0,1:T(2,128)(2,1)S(1)}, u32[]{:S(2)}, u32[]{:S(2)}) collective-permute-start(bf16[64,2]{0,1:T(2,128)(2,1)S(1)} %fusion.44), channel_id=1, source_target_pairs={{16,0},{20,4},{24,8},{28,12},{0,16},{4,20},{8,24},{12,28},{17,1},{... | collective-permute-start | bytes 776 | tf_op jit(solution)/shard_map/ppermute | solution.py:15
  14.0 1.3 collective-permute-start.2
  15.4 1.6 %collective-permute-start = (bf16[64,2]{0,1:T(2,128)(2,1)S(1)}, bf16[64,2]{0,1:T(2,128)(2,1)S(1)}, u32[]{:S(2)}, u32[]{:S(2)}) collective-permute-start(bf16[64,2]{0,1:T(2,128)(2,1)S(1)} %fusion.43), channel_id=1, source_target_pairs={{28,0},{0,4},{4,8},{8,12},{12,16},{16,20},{20,24},{24,28},{29,1},{... | collective-permute-start | bytes 776 | tf_op jit(solution)/shard_map/ppermute | solution.py:15
  16.9 0.0 copy-done
  16.9 0.2 convolution_convert_fusion.1
  17.1 3.6 %collective-permute-start.5 = (bf16[64,512]{1,0:T(8,128)(2,1)S(1)}, bf16[64,512]{1,0:T(8,128)(2,1)S(1)}, u32[]{:S(2)}, u32[]{:S(2)}) collective-permute-start(bf16[64,512]{1,0:T(8,128)(2,1)S(1)} %convolution_convert_fusion.1), channel_id=1, source_target_pairs={{12,0},{16,4},{20,8},{24,12},{28,16},{0,20},{4,24},{8,28},{13,1},{... | collective-permute-start | bytes 196616 | tf_op jit(solution)/shard_map/ppermute | solution.py:15
  20.7 0.2 convolution_convert_fusion.2
  20.9 0.4 collective-permute-start.4
  21.3 0.2 convolution_convert_fusion.4
  21.4 0.2 convolution_convert_fusion.3
  21.6 0.0 collective-permute-done.1
  21.6 0.3 collective-permute-start.3
  21.9 0.0 collective-permute-done.2
  21.9 0.0 collective-permute-done
  22.0 0.1 maximum_convert_fusion
  22.0 0.6 collective-permute-done.5
  22.6 4.2 %collective-permute-done.4 = bf16[64,512]{1,0:T(8,128)(2,1)S(1)} collective-permute-done((bf16[64,512]{1,0:T(8,128)(2,1)S(1)}, bf16[64,512]{1,0:T(8,128)(2,1)S(1)}, u32[]{:S(2)}, u32[]{:S(2)}) %collective-permute-start.4) | collective-permute-done | bytes 65568 | tf_op jit(solution)/shard_map/ppermute | solution.py:15
  26.8 1.9 %collective-permute-done.3 = bf16[64,512]{1,0:T(8,128)(2,1)S(1)} collective-permute-done((bf16[64,512]{1,0:T(8,128)(2,1)S(1)}, bf16[64,512]{1,0:T(8,128)(2,1)S(1)}, u32[]{:S(2)}, u32[]{:S(2)}) %collective-permute-start.3) | collective-permute-done | bytes 65568 | tf_op jit(solution)/shard_map/ppermute | solution.py:15
  28.7 0.9 convolution_convert_fusion
  29.6 0.0 all-gather.3.cloned.1.call-update
  29.6 0.0 reduce-scatter.2.cloned.1.call-start
  29.7 1.3 dynamic_slice.3
  31.0 0.6 fusion.47
  31.6 0.0 all-gather.5.cloned.1.call-done
  31.6 12.6 %fusion.51 = (f32[256]{0:T(256)S(1)}, f32[256,4096]{1,0:T(8,128)}) fusion(bf16[256,2048]{1,0:T(8,128)(2,1)} %all-gather.5.cloned.1.call-done, bf16[2048,4096]{1,0:T(8,128)(2,1)} %param.9), kind=kOutput, calls=%fused_computation.112 | convolution fusion | flops 4296015872 | bytes 22021120 | tf_op jit(solution)/shard_map/dot_general | solution.py:65
  44.3 0.0 copy-start.1
  44.3 0.0 copy-start.2
  44.3 3.7 %all-gather.3.cloned.1.call-done = bf16[256,2048]{1,0:T(8,128)(2,1)} async-done(((bf16[256,512]{1,0:T(8,128)(2,1)}), bf16[256,2048]{1,0:T(8,128)(2,1)}) %all-gather.3.cloned.1.call-update) | async-done | bytes 1048592 | tf_op jit(solution)/shard_map/all_gather | solution.py:61
  48.0 12.6 %fusion.50 = (f32[256]{0:T(256)S(1)}, f32[256,4096]{1,0:T(8,128)}) fusion(bf16[256,2048]{1,0:T(8,128)(2,1)} %all-gather.3.cloned.1.call-done, bf16[2048,4096]{1,0:T(8,128)(2,1)} %param.9), kind=kOutput, calls=%fused_computation.111 | convolution fusion | flops 4296015872 | bytes 22021120 | tf_op jit(solution)/shard_map/dot_general | solution.py:64
  60.5 5.8 %all-reduce.1 = (f32[256]{0:T(256)S(1)}, f32[256]{0:T(256)S(1)}) all-reduce(f32[256]{0:T(256)S(1)} %get-tuple-element.36, f32[256]{0:T(256)S(1)} %get-tuple-element.38), channel_id=1, replica_groups=mesh['tok'=8,'voc'=4] {'voc'}, use_global_device_ids=true, to_apply=%region_6.7 | all-reduce | flops 512 | bytes 4096 | tf_op jit(solution)/shard_map/pmax | solution.py:69
  66.4 0.0 copy-done.1
  66.4 0.0 copy-done.2
  66.4 5.6 %multiply_reduce_fusion = (f32[256]{0:T(256)S(1)}, f32[256]{0:T(256)S(1)}, f32[256]{0:T(256)S(1)}, f32[256]{0:T(256)S(1)}, f32[256]{0:T(256)S(1)}) fusion(f32[256,4096]{1,0:T(8,128)} %get-tuple-element.37, f32[256,4096]{1,0:T(8,128)} %get-tuple-element.39, f32[256]{0:T(256)S(1)} %get-tuple-element.16, s32[4096]{0:T(1024)S(1)} %copy-done.1, ...), kind=kLoop, calls=%fused_computation.7 | loop fusion | flops 12581632 | bytes 8413184 | tf_op jit(solution)/shard_map/reduce_sum | solution.py:78
  72.0 5.9 %all-reduce = (f32[256]{0:T(256)S(1)}, f32[256]{0:T(256)S(1)}, f32[256]{0:T(256)S(1)}, f32[256]{0:T(256)S(1)}, f32[256]{0:T(256)S(1)}) all-reduce(f32[256]{0:T(256)S(1)} %get-tuple-element.6, f32[256]{0:T(256)S(1)} %get-tuple-element.4, f32[256]{0:T(256)S(1)} %get-tuple-element.5, ...), channel_id=1, replica_groups=mesh['tok'=8,'voc'=4] {'voc'}, use_global_device_ids=true, to_apply=%region_16.17 | all-reduce | flops 1280 | bytes 10240 | tf_op jit(solution)/shard_map/psum | solution.py:74
  77.9 1.2 broadcast_add_fusion
  79.1 15.3 %convolution_bitcast_fusion = f32[2048,256]{0,1:T(8,128)} fusion(bf16[2048,4096]{1,0:T(8,128)(2,1)} %param.9, f32[256,4096]{1,0:T(8,128)} %get-tuple-element.37, f32[256,4096]{1,0:T(8,128)} %get-tuple-element.39, f32[256]{0:T(256)S(1)} %get-tuple-element.14, f32[256]{0:T(256)S(1)} %get-tuple-element.13, f32[256]{0:T(256)S(1)} %get-tuple-element.26, ...), kind=kOutput, calls=%fused_computation.11 | convolution fusion | flops 4306501632 | bytes 27286528 | tf_op jit(solution)/shard_map/dot_general | solution.py:96
  94.4 0.0 reduce-scatter.2.cloned.1.call-update
  94.4 32.7 %reduce-scatter.2.cloned.1.call-done = f32[512,256]{0,1:T(8,128)} async-done(((f32[2048,256]{0,1:T(8,128)}), f32[512,256]{0,1:T(8,128)}) %reduce-scatter.2.cloned.1.call-update) | async-done | bytes 524304 | tf_op jit(solution)/shard_map/reduce_scatter | solution.py:95
  127.1 1.8 %fusion.14 = bf16[256,512]{1,0:T(8,128)(2,1)} fusion(f32[512,256]{0,1:T(8,128)} %reduce-scatter.2.cloned.1.call-done), kind=kLoop, calls=%fused_computation.26 | loop fusion | flops 262144 | bytes 786432 | tf_op jit(solution)/shard_map/convert_element_type | solution.py:103
  (9 shorter events, 0.1 us)
Async XLA Ops:
  7.2 9.8 %copy-start = (bf16[256,512]{1,0:T(8,128)(2,1)S(1)}, bf16[256,512]{1,0:T(8,128)(2,1)}, u32[]{:S(2)}) copy-start(bf16[256,512]{1,0:T(8,128)(2,1)} %param.7) | copy-start | bytes 786436
  7.2 24.5 %all-gather.5.cloned.1.call-start = ((), (), s32[]{:S(2)}) async-start(), calls=%async_computation.2 | async-start | bytes 1310720 | tf_op jit(solution)/shard_map/all_gather | solution.py:62
  7.9 40.0 %all-gather.3.cloned.1.call-start = ((), (), s32[]{:S(2)}) async-start(), calls=%async_computation.1 | async-start | bytes 1310720 | tf_op jit(solution)/shard_map/all_gather | solution.py:61
  9.9 11.8 %collective-permute-start.1 = (bf16[64,2]{0,1:T(2,128)(2,1)S(1)}, bf16[64,2]{0,1:T(2,128)(2,1)S(1)}, u32[]{:S(2)}, u32[]{:S(2)}) collective-permute-start(bf16[64,2]{0,1:T(2,128)(2,1)S(1)} %fusion.44), channel_id=1, source_target_pairs={{16,0},{20,4},{24,8},{28,12},{0,16},{4,20},{8,24},{12,28},{17,1},{... | collective-permute-start | bytes 776 | tf_op jit(solution)/shard_map/ppermute | solution.py:15
  14.0 8.0 %collective-permute-start.2 = (bf16[64,2]{0,1:T(2,128)(2,1)S(1)}, bf16[64,2]{0,1:T(2,128)(2,1)S(1)}, u32[]{:S(2)}, u32[]{:S(2)}) collective-permute-start(bf16[64,2]{0,1:T(2,128)(2,1)S(1)} %fusion.45), channel_id=1, source_target_pairs={{12,0},{16,4},{20,8},{24,12},{28,16},{0,20},{4,24},{8,28},{13,1},{... | collective-permute-start | bytes 776 | tf_op jit(solution)/shard_map/ppermute | solution.py:15
  15.4 6.6 %collective-permute-start = (bf16[64,2]{0,1:T(2,128)(2,1)S(1)}, bf16[64,2]{0,1:T(2,128)(2,1)S(1)}, u32[]{:S(2)}, u32[]{:S(2)}) collective-permute-start(bf16[64,2]{0,1:T(2,128)(2,1)S(1)} %fusion.43), channel_id=1, source_target_pairs={{28,0},{0,4},{4,8},{8,12},{12,16},{16,20},{20,24},{24,28},{29,1},{... | collective-permute-start | bytes 776 | tf_op jit(solution)/shard_map/ppermute | solution.py:15
  17.1 5.5 %collective-permute-start.5 = (bf16[64,512]{1,0:T(8,128)(2,1)S(1)}, bf16[64,512]{1,0:T(8,128)(2,1)S(1)}, u32[]{:S(2)}, u32[]{:S(2)}) collective-permute-start(bf16[64,512]{1,0:T(8,128)(2,1)S(1)} %convolution_convert_fusion.1), channel_id=1, source_target_pairs={{12,0},{16,4},{20,8},{24,12},{28,16},{0,20},{4,24},{8,28},{13,1},{... | collective-permute-start | bytes 196616 | tf_op jit(solution)/shard_map/ppermute | solution.py:15
  20.9 5.9 %collective-permute-start.4 = (bf16[64,512]{1,0:T(8,128)(2,1)S(1)}, bf16[64,512]{1,0:T(8,128)(2,1)S(1)}, u32[]{:S(2)}, u32[]{:S(2)}) collective-permute-start(bf16[64,512]{1,0:T(8,128)(2,1)S(1)} %convolution_convert_fusion.2), channel_id=1, source_target_pairs={{16,0},{20,4},{24,8},{28,12},{0,16},{4,20},{8,24},{12,28},{17,1},{... | collective-permute-start | bytes 196616 | tf_op jit(solution)/shard_map/ppermute | solution.py:15
  21.6 7.0 %collective-permute-start.3 = (bf16[64,512]{1,0:T(8,128)(2,1)S(1)}, bf16[64,512]{1,0:T(8,128)(2,1)S(1)}, u32[]{:S(2)}, u32[]{:S(2)}) collective-permute-start(bf16[64,512]{1,0:T(8,128)(2,1)S(1)} %convolution_convert_fusion.3), channel_id=1, source_target_pairs={{28,0},{0,4},{4,8},{8,12},{12,16},{16,20},{20,24},{24,28},{29,1},{... | collective-permute-start | bytes 196616 | tf_op jit(solution)/shard_map/ppermute | solution.py:15
  29.6 97.5 %reduce-scatter.2.cloned.1.call-start = ((), (), s32[]{:S(2)}) async-start(), calls=%async_computation.3 | async-start | bytes 2621440 | tf_op jit(solution)/shard_map/reduce_scatter | solution.py:95
  44.3 22.1 %copy-start.1 = (s32[4096]{0:T(1024)S(1)}, s32[4096]{0:T(1024)}, u32[]{:S(2)}) copy-start(s32[4096]{0:T(1024)} %param.10) | copy-start | bytes 49156
  44.3 22.1 %copy-start.2 = (s32[256]{0:T(256)S(1)}, s32[256]{0:T(256)}, u32[]{:S(2)}) copy-start(s32[256]{0:T(256)} %param.11) | copy-start | bytes 3076
Sparse Core Ops, SparseCore 0:
  9.5 19.4 all-gather.4
  31.2 16.6 all-gather.2
  94.5 32.5 reduce-scatter.1
where the time goes:
time: 136 us; the launch traced here: 135 us
  waiting for transfers between devices  43.7 us (32%)
  matrix products  42.1 us (31%)
  between operations  13.8 us (10%)
  blocking collectives  11.8 us (9%)
  starting transfers between devices  11.4 us (8%)
  other arithmetic  11.2 us (8%)
    reduce_scatter x1, waiting for transfers between devices, per_device(): lax.psum_scatter(lax.dot_general(head, grad_logit, (((1,), (1,)), ((), ()...  32.7 us
    dot_general x1, matrix products, per_device(): lax.dot_general(head, grad_logit, (((1,), (1,)), ((), ())), preferred_ele...  15.3 us
    dot_general x1, matrix products, per_device(): jnp.dot(drafter_full, head, preferred_element_type=jnp.float32)  12.6 us
    dot_general x1, matrix products, per_device(): jnp.dot(teacher_full, head, preferred_element_type=jnp.float32)  12.6 us
    ppermute x6, starting transfers between devices, shifted(): return lax.ppermute(block, axis, route)  11.3 us
    ppermute x6, waiting for transfers between devices, shifted(): return lax.ppermute(block, axis, route)  6.63 us
    psum x1, blocking collectives, per_device(): lax.psum((jnp.sum(teach_exp, axis=1), jnp.sum(draft_exp, axis=1), jnp.sum...  5.92 us
    pmax x1, blocking collectives, per_device(): lax.pmax((jnp.max(teach_logit, axis=1), jnp.max(draft_logit, axis=1)), 'v...  5.85 us
  transfers between devices with their start and end apart: 9, of which 5 were waited for; matrix products, arithmetic and copies ran while one was open for 13% of the time, Pallas kernels for 0%

commit v1 on v0

v1 whole, which is shorter than its diff:
```python
import functools

import jax
import jax.numpy as jnp
from jax import lax
from jax.experimental import pallas as pl
from jax.experimental.pallas import tpu as pltpu
from jax.sharding import PartitionSpec as P

REACH = 4
CORES = 2
PAD = 8

loss_scale = 16.0

VM = pl.BlockSpec(memory_space=pltpu.VMEM)
SM = pl.BlockSpec(memory_space=pltpu.SMEM)


def call(body, outs, specs, name, flops=0, mib=8):
    return pl.pallas_call(
        body,
        out_shape=outs,
        in_specs=specs,
        out_specs=jax.tree.map(lambda _: VM, outs),
        name=name,
        cost_estimate=pl.CostEstimate(flops=flops, transcendentals=0, bytes_accessed=0),
        compiler_params=pltpu.CompilerParams(vmem_limit_bytes=mib << 20),
    )


def shape(dims, dtype=jnp.float32):
    return jax.ShapeDtypeStruct(dims, dtype)


def shifts_of(tok_size):
    return [0, 1, tok_size // 2, tok_size // 2 + 1]


def pack_body(tok_size, dest_ref, rows_ref, *outs):
    rows = rows_ref.shape[0]
    capacity = rows // REACH
    me = lax.axis_index("tok")
    dest = dest_ref[...]
    slot = lax.broadcasted_iota(jnp.int32, (capacity, rows), 0)
    for out, shift in zip(outs, shifts_of(tok_size)):
        low = lax.rem(me + shift, tok_size) * rows
        inside = (dest >= low) & (dest < low + rows)
        first = jnp.min(jnp.where(inside, dest - low, rows), axis=1, keepdims=True)
        place = jnp.where(inside, dest - low - first, -1)
        select = jnp.where(slot == place, 1.0, 0.0).astype(jnp.bfloat16)
        out[:capacity] = jnp.dot(select, rows_ref[...], preferred_element_type=jnp.float32).astype(jnp.bfloat16)
        out[capacity:] = jnp.broadcast_to(first.astype(jnp.float32), (PAD, out.shape[1])).astype(jnp.bfloat16)


def unpack_body(*refs):
    *parts, out = refs
    rows = out.shape[0]
    capacity = rows // REACH
    slot = lax.broadcasted_iota(jnp.int32, (rows, capacity), 0)
    rank = lax.broadcasted_iota(jnp.int32, (rows, capacity), 1)
    total = jnp.zeros(out.shape, jnp.float32)
    for part in parts:
        first = part[capacity:, :capacity].astype(jnp.float32).astype(jnp.int32)[:1]
        select = jnp.where(slot == rank + first, 1.0, 0.0).astype(jnp.bfloat16)
        total += jnp.dot(select, part[:capacity], preferred_element_type=jnp.float32)
    out[...] = total.astype(out.dtype)


def joined(mine, other, buf):
    width = mine.shape[1]
    core = lax.rem(lax.axis_index("voc"), CORES)
    buf[:, pl.ds(pl.multiple_of(core * width, width), width)] = mine[...]
    buf[:, pl.ds(pl.multiple_of((1 - core) * width, width), width)] = other[...]


def chip_rows(step, chips, depth):
    chip = lax.rem(lax.axis_index("voc") // CORES + chips - step, chips)
    return pl.ds(pl.multiple_of(chip * depth, depth), depth)


def blocks_of(width):
    size = min(1024, width)
    return [slice(i, i + size) for i in range(0, width, size)]


def first_body(step, chips, mine, other, head, out, buf):
    joined(mine, other, buf)
    rows = chip_rows(step, chips, buf.shape[1])
    for cols in blocks_of(out.shape[1]):
        out[:, cols] = jnp.dot(buf[...], head[rows, cols], preferred_element_type=jnp.float32)


def more_body(step, chips, mine, other, head, acc, out, buf):
    joined(mine, other, buf)
    rows = chip_rows(step, chips, buf.shape[1])
    for cols in blocks_of(out.shape[1]):
        out[:, cols] = acc[:, cols] + jnp.dot(buf[...], head[rows, cols], preferred_element_type=jnp.float32)


def lanes(block):
    return [block[:, i : i + 128] for i in range(0, block.shape[1], 128)]


def as_row(column):
    return jnp.broadcast_to(column, (column.shape[0], 8)).T[:1]


def as_column(row):
    return jnp.broadcast_to(row, (8, row.shape[1])).T[:, :1]


def draft_body(step, chips, mine, other, head, acc, ids, wanted, out, stats, buf):
    joined(mine, other, buf)
    depth = chip_rows(step, chips, buf.shape[1])
    count = out.shape[0]
    target = jnp.broadcast_to(as_column(wanted[...]), (count, 128))
    top = jnp.full((count, 128), -jnp.inf, jnp.float32)
    total = jnp.zeros((count, 128), jnp.float32)
    hits = jnp.zeros((count, 128), jnp.float32)
    picked = jnp.zeros((count, 128), jnp.float32)
    for cols in blocks_of(out.shape[1]):
        out[:, cols] = acc[:, cols] + jnp.dot(buf[...], head[depth, cols], preferred_element_type=jnp.float32)
        block = lanes(out[:, cols])
        above = functools.reduce(jnp.maximum, block, top)
        total = total * jnp.exp(top - above)
        top = above
        for piece, ident in zip(block, lanes(ids[:, cols])):
            total += jnp.exp(piece - top)
            same = target == ident
            hits += jnp.where(same, 1.0, 0.0)
            picked += jnp.where(same, piece, 0.0)
    peak = jnp.max(top, axis=1, keepdims=True)
    total = jnp.sum(total * jnp.exp(top - peak), axis=1, keepdims=True)
    stats[0:1] = as_row(peak)
    stats[1:2] = as_row(total)
    stats[2:3] = as_row(jnp.sum(picked, axis=1, keepdims=True))
    stats[3:4] = as_row(jnp.sum(hits, axis=1, keepdims=True))
    stats[4:] = jnp.zeros((4, count), jnp.float32)


def teach_body(step, chips, mine, other, head, acc, draft, known, out, stats, buf):
    joined(mine, other, buf)
    depth = chip_rows(step, chips, buf.shape[1])
    count = out.shape[0]
    top = jnp.full((count, 128), -jnp.inf, jnp.float32)
    total = jnp.zeros((count, 128), jnp.float32)
    cross = jnp.zeros((count, 128), jnp.float32)
    for cols in blocks_of(out.shape[1]):
        out[:, cols] = acc[:, cols] + jnp.dot(buf[...], head[depth, cols], preferred_element_type=jnp.float32)
        block = lanes(out[:, cols])
        above = functools.reduce(jnp.maximum, block, top)
        scale = jnp.exp(top - above)
        total = total * scale
        cross = cross * scale
        top = above
        for piece, drafted in zip(block, lanes(draft[:, cols])):
            weight = jnp.exp(piece - top)
            total += weight
            cross += weight * (piece - drafted)
    peak = jnp.max(top, axis=1, keepdims=True)
    scale = jnp.exp(top - peak)
    stats[0:4] = known[0:4]
    stats[4:5] = as_row(peak)
    stats[5:6] = as_row(jnp.sum(total * scale, axis=1, keepdims=True))
    stats[6:7] = as_row(jnp.sum(cross * scale, axis=1, keepdims=True))
    stats[7:] = jnp.zeros((1, count), jnp.float32)


def feature_rows(step, chips, other_core, width):
    me = lax.axis_index("voc")
    chip = lax.rem(me // CORES + step, chips)
    core = lax.rem(me, CORES)
    core = 1 - core if other_core else core
    return pl.ds(pl.multiple_of((chip * CORES + core) * width, width), width)


def grad_body(step, chips, parts, width, counts, *refs):
    every = [ref[...] for ref in refs[:parts]]
    draft, teach, ids, wanted, head, loss, grads, out = refs[parts:]
    count = draft.shape[0]
    here = [(s[0:1], s[1:2], s[2:3], s[3:4], s[4:5], s[5:6], s[6:7]) for s in every]
    draft_max = functools.reduce(jnp.maximum, [s[0] for s in here])
    teach_max = functools.reduce(jnp.maximum, [s[4] for s in here])
    draft_total = sum(s[1] * jnp.exp(s[0] - draft_max) for s in here)
    teach_total = sum(s[5] * jnp.exp(s[4] - teach_max) for s in here)
    cross = sum(s[6] * jnp.exp(s[4] - teach_max) for s in here)
    picked = sum(s[2] for s in here)
    hits = sum(s[3] for s in here)
    draft_lse = draft_max + jnp.log(draft_total)
    teach_lse = teach_max + jnp.log(teach_total)
    slots = lax.broadcasted_iota(jnp.int32, (1, count), 1)
    valid = slots < counts[0, lax.axis_index("tok")]
    row_loss = cross / teach_total - teach_lse + draft_lse + hits * (draft_lse - picked)
    loss[...] = jnp.where(valid, row_loss, 0.0)
    target = jnp.broadcast_to(as_column(wanted[...]), (count, 128))
    keep = jnp.where(valid, 1.0, 0.0)
    draft_shift = jnp.broadcast_to(as_column(draft_lse), (count, 128))
    teach_shift = jnp.broadcast_to(as_column(teach_lse), (count, 128))
    factor = jnp.broadcast_to(as_column(keep * (1.0 + hits)), (count, 128))
    keep = jnp.broadcast_to(as_column(keep), (count, 128))
    rows = feature_rows(step, chips, True, width)
    total = jnp.zeros(out.shape, jnp.float32)
    for cols in blocks_of(draft.shape[1]):
        for start in range(cols.start, cols.stop, 128):
            at = slice(start, start + 128)
            value = factor * jnp.exp(draft[:, at] - draft_shift) - keep * jnp.exp(teach[:, at] - teach_shift)
            value = value - jnp.where(target == ids[:, at], keep, 0.0)
            grads[:, at] = value.astype(jnp.bfloat16)
        total += lax.dot_general(
            grads[:, cols], head[rows, cols], (((1,), (1,)), ((), ())), preferred_element_type=jnp.float32
        )
    out[...] = total.astype(out.dtype)


def slice_body(step, chips, other_core, width, grads, head, out):
    rows = feature_rows(step, chips, other_core, width)
    out[...] = lax.dot_general(
        grads[...], head[rows, :], (((1,), (1,)), ((), ())), preferred_element_type=jnp.float32
    ).astype(out.dtype)


def per_device(teacher_rows, drafter_rows, head, fr_ids, targets, dest_index, counts):
    tok_size = lax.axis_size("tok")
    voc_size = lax.axis_size("voc")
    chips = voc_size // CORES
    rows, width = teacher_rows.shape
    features, columns = head.shape
    capacity = rows // REACH
    half = CORES * width
    flops = 2 * rows * columns * width

    def over_tok(block, distance):
        return lax.ppermute(block, "tok", [(i, (i + distance) % tok_size) for i in range(tok_size)])

    def over_chips(block, step):
        return lax.ppermute(block, "voc", [(i, (i + step * CORES) % voc_size) for i in range(voc_size)])

    def over_cores(block):
        return lax.ppermute(block, "voc", [(i, i + 1 - 2 * (i % CORES)) for i in range(voc_size)])

    head = pltpu.with_memory_space_constraint(head, pltpu.VMEM)
    ids = fr_ids.reshape(1, columns)
    wanted = targets.reshape(1, rows)

    parts = call(
        functools.partial(pack_body, tok_size),
        [shape((capacity + PAD, width), jnp.bfloat16)] * REACH,
        [VM, VM],
        "pack",
    )(dest_index.reshape(1, rows), teacher_rows)
    parts = [part if shift == 0 else over_tok(part, shift) for part, shift in zip(parts, shifts_of(tok_size))]
    moved = call(unpack_body, shape((rows, width), jnp.bfloat16), [VM] * REACH, "unpack")(*parts)

    def gathered(block):
        mine = [block] + [over_chips(block, step) for step in range(1, chips)]
        return [(piece, over_cores(piece)) for piece in mine]

    def partial(pairs, name):
        acc = None
        buf = [pltpu.VMEM((rows, half), jnp.bfloat16)]
        for step, (mine, other) in enumerate(pairs):
            body = first_body if acc is None else more_body
            acc = pl.pallas_call(
                functools.partial(body, step, chips),
                out_shape=shape((rows, columns)),
                in_specs=[VM] * (3 if acc is None else 4),
                out_specs=VM,
                scratch_shapes=buf,
                name=name + str(step),
                cost_estimate=pl.CostEstimate(flops=2 * flops, transcendentals=0, bytes_accessed=0),
                compiler_params=pltpu.CompilerParams(vmem_limit_bytes=12 << 20),
            )(mine, other, head, *([] if acc is None else [acc]))
        return acc

    def last(body, pair, acc, extra, name):
        return pl.pallas_call(
            functools.partial(body, chips - 1, chips),
            out_shape=[shape((rows, columns)), shape((8, rows))],
            in_specs=[VM] * (4 + len(extra)),
            out_specs=[VM, VM],
            scratch_shapes=[pltpu.VMEM((rows, half), jnp.bfloat16)],
            name=name,
            cost_estimate=pl.CostEstimate(flops=3 * flops, transcendentals=0, bytes_accessed=0),
            compiler_params=pltpu.CompilerParams(vmem_limit_bytes=12 << 20),
        )(*pair, head, acc, *extra)

    draft_pairs = gathered(drafter_rows)
    teach_pairs = gathered(moved)
    draft, known = last(draft_body, draft_pairs[-1], partial(draft_pairs[:-1], "draft"), (ids, wanted), "draft_last")
    teach, stats = last(teach_body, teach_pairs[-1], partial(teach_pairs[:-1], "teach"), (draft, known), "teach_last")

    every = [stats] + [over_chips(stats, step) for step in range(1, chips)]
    every = every + [over_cores(piece) for piece in every]

    step = 1 % chips
    loss, grads, sent = call(
        functools.partial(grad_body, step, chips, len(every), width),
        [shape((1, rows)), shape((rows, columns), jnp.bfloat16), shape((rows, width), jnp.bfloat16)],
        [SM] + [VM] * (len(every) + 5),
        "grad",
        2 * flops,
    )(counts.reshape(1, tok_size), *every, draft, teach, ids, wanted, head)

    def grad_slice(step, other_core, dtype):
        return call(
            functools.partial(slice_body, step, chips, other_core, width),
            shape((rows, width), dtype),
            [VM, VM],
            "slice%d_%d" % (step, other_core),
            flops,
        )(grads, head)

    arrived = []
    for step in range(1, chips):
        if step > 1:
            sent = grad_slice(step, True, jnp.bfloat16)
        own = grad_slice(step, False, jnp.float32)
        pair = (own + over_cores(sent).astype(jnp.float32)).astype(jnp.bfloat16)
        arrived.append(over_chips(pair, step))
    total = grad_slice(0, False, jnp.float32) + over_cores(grad_slice(0, True, jnp.bfloat16)).astype(jnp.float32)
    for piece in arrived:
        total = total + piece.astype(jnp.float32)
    return loss.reshape(rows), (loss_scale * total).astype(jnp.bfloat16)


def solution(mesh):
    return jax.shard_map(
        per_device,
        mesh=mesh,
        in_specs=(
            P("tok", "voc"),
            P("tok", "voc"),
            P(None, "voc"),
            P("voc"),
            P("tok"),
            P("tok"),
            P(),
        ),
        out_specs=(P("tok"), P("tok", "voc")),
        check_vma=False,
    )
```

time: 136 us -> 61.8 us (0.45)
  matrix products: 42.1 us -> 0 us
  waiting for transfers between devices: 43.7 us -> 14.4 us
  Pallas kernels: 0 us -> 20.5 us
  between operations: 13.8 us -> 0.79 us
  blocking collectives: 11.8 us -> 0 us
  other arithmetic: 11.2 us -> 0.89 us
  local copies, waits for them, and re-layouts: 1.31 us -> 11.6 us
  starting transfers between devices: 11.4 us -> 13.4 us
    dot_general x8 -> x0, matrix products: 42.1 us -> none  [the longest x1 15.3 us: per_device(): lax.dot_general(head, grad_logit, (((1,), (1,)), ((), ())), preferred_ele...]
    reduce_scatter x1 -> x0, waiting for transfers between devices: 32.7 us -> none  [per_device(): lax.psum_scatter(lax.dot_general(head, grad_logit, (((1,), (1,)), ((), ()...]
    pallas_call x0 -> x10, Pallas kernels: none -> 20.5 us  [the longest x2 6.94 us: last(): pl.pallas_call(functools.partial(body, chips - 1, chips), out_shape=[shap...]
    unnamed x6 -> x16, local copies, waits for them, and re-layouts: 0.02 us -> 11.6 us
    ppermute x6 -> x15, waiting for transfers between devices: 6.63 us -> 14.4 us  [the longest x4 7.74 us: over_chips(): lax.ppermute(block, 'voc', [(i, (i + step * CORES) % voc_size) for i in r...]
    reduce_sum x3 -> x0, other arithmetic: 6.68 us -> none  [the longest x1 5.56 us: per_device(): jnp.sum(teach_exp * (teach_logit - draft_logit), axis=1)]
    psum x1 -> x0, blocking collectives: 5.92 us -> none  [per_device(): lax.psum((jnp.sum(teach_exp, axis=1), jnp.sum(draft_exp, axis=1), jnp.sum...]
    pmax x1 -> x0, blocking collectives: 5.85 us -> none  [per_device(): lax.pmax((jnp.max(teach_logit, axis=1), jnp.max(draft_logit, axis=1)), 'v...]
  transfers between devices with their start and end apart: 9 -> 15, of which waited for: 5 -> 6; matrix products, arithmetic and copies ran while one was open for 13% -> 0% of each run, Pallas kernels for 0% -> 21%
where the time goes in v1:
time: 61.8 us; the launch traced here: 61.5 us
  Pallas kernels  20.5 us (33%)
  waiting for transfers between devices  14.4 us (23%)
  starting transfers between devices  13.4 us (22%)
  local copies, waits for them, and re-layouts  11.6 us (19%)
  other arithmetic  0.89 us (1%)
  between operations  0.79 us (1%)
    unnamed x16, local copies, waits for them, and re-layouts  11.6 us
    ppermute x4, waiting for transfers between devices, over_chips(): lax.ppermute(block, 'voc', [(i, (i + step * CORES) % voc_size) for i in r...  7.74 us
    pallas_call x2, Pallas kernels, last(): pl.pallas_call(functools.partial(body, chips - 1, chips), out_shape=[shap...  6.94 us
    ppermute x4, starting transfers between devices, over_chips(): lax.ppermute(block, 'voc', [(i, (i + step * CORES) % voc_size) for i in r...  6.74 us
    ppermute x3, starting transfers between devices, over_tok(): lax.ppermute(block, 'tok', [(i, (i + distance) % tok_size) for i in range...  5.45 us
    ppermute x3, waiting for transfers between devices, over_tok(): lax.ppermute(block, 'tok', [(i, (i + distance) % tok_size) for i in range...  5.44 us
    pallas_call x2, Pallas kernels, partial(): pl.pallas_call(functools.partial(body, step, chips), out_shape=shape((row...  4.75 us
    pallas_call x1, Pallas kernels, per_device(): call(functools.partial(grad_body, step, chips, len(every), width), [shape...  4.15 us
  transfers between devices with their start and end apart: 15, of which 6 were waited for; matrix products, arithmetic and copies ran while one was open for 0% of the time, Pallas kernels for 21%

profile of v1, /device:TPU:0, one launch (start us, length us, event | category | flops | bytes accessed | tf_op | source)
XLA Modules:
  0.0 61.5 jit_solution(5518394696724234533)
XLA Ops:
  0.6 3.0 %collective-permute-start.6 = (bf16[256,512]{1,0:T(8,128)(2,1)}, bf16[256,512]{1,0:T(8,128)(2,1)S(1)}, u32[]{:S(2)}, u32[]{:S(2)}) collective-permute-start(bf16[256,512]{1,0:T(8,128)(2,1)} %mine.1), channel_id=1, source_target_pairs={{0,2},{1,3},{2,0},{3,1},{4,6},{5,7},{6,4},{7,5},{8,10},{9,11},{10,... | collective-permute-start | bytes 786440 | tf_op jit(solution)/shard_map/ppermute | solution.py:237
  3.7 0.0 collective-permute-start.8
  3.7 0.0 copy-start.3
  3.7 0.9 %copy-done.3 = bf16[256,512]{1,0:T(8,128)(2,1)S(1)} copy-done((bf16[256,512]{1,0:T(8,128)(2,1)S(1)}, bf16[256,512]{1,0:T(8,128)(2,1)}, u32[]{:S(2)}) %copy-start.3) | copy-done | bytes 262168
  4.6 0.0 copy-start.6
  4.6 0.7 %copy-done.6 = s32[256]{0:T(256)S(1)} copy-done((s32[256]{0:T(256)S(1)}, s32[256]{0:T(256)}, u32[]{:S(2)}) %copy-start.6) | copy-done | bytes 1048
  5.3 0.4 pack.1
  5.7 1.6 %collective-permute-start = (bf16[72,512]{1,0:T(8,128)(2,1)S(1)}, bf16[72,512]{1,0:T(8,128)(2,1)S(1)}, u32[]{:S(2)}, u32[]{:S(2)}) collective-permute-start(bf16[72,512]{1,0:T(8,128)(2,1)S(1)} %get-tuple-element.14), channel_id=1, source_target_pairs={{0,4},{4,8},{8,12},{12,16},{16,20},{20,24},{24,28},{28,0},{1,5},{5... | collective-permute-start | bytes 221192 | tf_op jit(solution)/shard_map/ppermute | solution.py:234
  7.3 2.6 %collective-permute-start.1 = (bf16[72,512]{1,0:T(8,128)(2,1)S(1)}, bf16[72,512]{1,0:T(8,128)(2,1)S(1)}, u32[]{:S(2)}, u32[]{:S(2)}) collective-permute-start(bf16[72,512]{1,0:T(8,128)(2,1)S(1)} %get-tuple-element.15), channel_id=1, source_target_pairs={{0,16},{4,20},{8,24},{12,28},{16,0},{20,4},{24,8},{28,12},{1,17},{... | collective-permute-start | bytes 221192 | tf_op jit(solution)/shard_map/ppermute | solution.py:234
  9.9 1.3 %collective-permute-start.2 = (bf16[72,512]{1,0:T(8,128)(2,1)S(1)}, bf16[72,512]{1,0:T(8,128)(2,1)S(1)}, u32[]{:S(2)}, u32[]{:S(2)}) collective-permute-start(bf16[72,512]{1,0:T(8,128)(2,1)S(1)} %get-tuple-element.16), channel_id=1, source_target_pairs={{0,20},{4,24},{8,28},{12,0},{16,4},{20,8},{24,12},{28,16},{1,21},{... | collective-permute-start | bytes 221192 | tf_op jit(solution)/shard_map/ppermute | solution.py:234
  11.2 2.5 %collective-permute-done.refs_1_ = bf16[72,512]{1,0:T(8,128)(2,1)S(1)} collective-permute-done((bf16[72,512]{1,0:T(8,128)(2,1)S(1)}, bf16[72,512]{1,0:T(8,128)(2,1)S(1)}, u32[]{:S(2)}, u32[]{:S(2)}) %collective-permute-start) | collective-permute-done | bytes 73760 | tf_op jit(solution)/shard_map/ppermute | solution.py:234
  13.7 2.1 %collective-permute-done.1.refs_2_ = bf16[72,512]{1,0:T(8,128)(2,1)S(1)} collective-permute-done((bf16[72,512]{1,0:T(8,128)(2,1)S(1)}, bf16[72,512]{1,0:T(8,128)(2,1)S(1)}, u32[]{:S(2)}, u32[]{:S(2)}) %collective-permute-start.1) | collective-permute-done | bytes 73760 | tf_op jit(solution)/shard_map/ppermute | solution.py:234
  15.8 0.8 %collective-permute-done.2.refs_3_ = bf16[72,512]{1,0:T(8,128)(2,1)S(1)} collective-permute-done((bf16[72,512]{1,0:T(8,128)(2,1)S(1)}, bf16[72,512]{1,0:T(8,128)(2,1)S(1)}, u32[]{:S(2)}, u32[]{:S(2)}) %collective-permute-start.2) | collective-permute-done | bytes 73760 | tf_op jit(solution)/shard_map/ppermute | solution.py:234
  16.6 0.4 unpack.1.mine
  17.0 0.6 collective-permute-start.3
  17.6 0.0 collective-permute-start.5
  17.6 0.0 collective-permute-done.6.mine
  17.7 0.5 collective-permute-start.7
  18.2 0.0 collective-permute-done.8.other
  18.2 0.0 copy-start
  18.2 5.8 %copy-done = bf16[2048,4096]{1,0:T(8,128)(2,1)S(1)} copy-done((bf16[2048,4096]{1,0:T(8,128)(2,1)S(1)}, bf16[2048,4096]{1,0:T(8,128)(2,1)}, u32[]{:S(2)}) %copy-start) | copy-done | bytes 16777240
  23.9 0.0 copy-start.2
  23.9 0.9 %copy-done.2 = bf16[256,512]{1,0:T(8,128)(2,1)S(1)} copy-done((bf16[256,512]{1,0:T(8,128)(2,1)S(1)}, bf16[256,512]{1,0:T(8,128)(2,1)}, u32[]{:S(2)}) %copy-start.2) | copy-done | bytes 262168
  24.9 0.0 copy-start.1
  24.9 2.4 %draft0.1.acc = f32[256,4096]{1,0:T(8,128)S(1)} custom-call(bf16[256,512]{1,0:T(8,128)(2,1)S(1)} %copy-done.2, bf16[256,512]{1,0:T(8,128)(2,1)S(1)} %collective-permute-done.8.other, bf16[2048,4096]{1,0:T(8,128)(2,1)S(1)} %copy-done), custom_call_target="tpu_custom_call" | custom-call | flops 2147483648 | tf_op jit(solution)/shard_map/draft0/pallas_call | solution.py:264
  27.3 0.0 copy-start.4
  27.3 0.0 copy-start.5
  27.3 0.0 collective-permute-done.3.mine
  27.3 0.1 collective-permute-start.4
  27.4 0.0 collective-permute-done.5.other
  27.4 3.3 %copy-done.1 = bf16[2048,4096]{1,0:T(8,128)(2,1)S(1)} copy-done((bf16[2048,4096]{1,0:T(8,128)(2,1)S(1)}, bf16[2048,4096]{1,0:T(8,128)(2,1)}, u32[]{:S(2)}) %copy-start.1) | copy-done | bytes 16777240
  30.7 2.4 %teach0.1.acc = f32[256,4096]{1,0:T(8,128)S(1)} custom-call(bf16[256,512]{1,0:T(8,128)(2,1)S(1)} %unpack.1.mine, bf16[256,512]{1,0:T(8,128)(2,1)S(1)} %collective-permute-done.5.other, bf16[2048,4096]{1,0:T(8,128)(2,1)S(1)} %copy-done.1), custom_call_target="tpu_custom_call" | custom-call | flops 2147483648 | tf_op jit(solution)/shard_map/teach0/pallas_call | solution.py:264
  33.0 0.0 collective-permute-done.7.other
  33.1 0.0 copy-done.4
  33.1 0.0 copy-done.5
  33.1 3.6 %draft_last.1 = (f32[256,4096]{1,0:T(8,128)S(1)}, f32[8,256]{1,0:T(8,128)S(1)}) custom-call(bf16[256,512]{1,0:T(8,128)(2,1)S(1)} %collective-permute-done.6.mine, bf16[256,512]{1,0:T(8,128)(2,1)S(1)} %collective-permute-done.7.other, bf16[2048,4096]{1,0:T(8,128)(2,1)S(1)} %copy-done.1, f32[256,4096]{1,0:T(8,128)S(1)} %draft0.1.acc, s32[1,4096]{1,0:T(1,128)S(1)} %bitcast.5, ...), custom_call_target="tpu_custom_call" | custom-call | flops 3221225472 | tf_op jit(solution)/shard_map/draft_last/pallas_call | solution.py:277
  36.7 0.0 collective-permute-done.4.other
  36.7 0.0 copy-start.7
  36.7 3.3 %teach_last.1 = (f32[256,4096]{1,0:T(8,128)S(1)}, f32[8,256]{1,0:T(8,128)S(1)}) custom-call(bf16[256,512]{1,0:T(8,128)(2,1)S(1)} %collective-permute-done.3.mine, bf16[256,512]{1,0:T(8,128)(2,1)S(1)} %collective-permute-done.4.other, bf16[2048,4096]{1,0:T(8,128)(2,1)S(1)} %copy-done.1, f32[256,4096]{1,0:T(8,128)S(1)} %teach0.1.acc, ...), custom_call_target="tpu_custom_call" | custom-call | flops 3221225472 | tf_op jit(solution)/shard_map/teach_last/pallas_call | solution.py:277
  40.0 1.5 %collective-permute-start.9 = (f32[8,256]{1,0:T(8,128)S(1)}, f32[8,256]{1,0:T(8,128)S(1)}, u32[]{:S(2)}, u32[]{:S(2)}) collective-permute-start(f32[8,256]{1,0:T(8,128)S(1)} %get-tuple-element.19.refs_0_), channel_id=1, source_target_pairs={{0,2},{1,3},{2,0},{3,1},{4,6},{5,7},{6,4},{7,5},{8,10},{9,11},{10,... | collective-permute-start | bytes 24584 | tf_op jit(solution)/shard_map/ppermute | solution.py:237
  41.6 0.0 collective-permute-start.10
  41.6 2.1 %collective-permute-done.9.refs_1_ = f32[8,256]{1,0:T(8,128)S(1)} collective-permute-done((f32[8,256]{1,0:T(8,128)S(1)}, f32[8,256]{1,0:T(8,128)S(1)}, u32[]{:S(2)}, u32[]{:S(2)}) %collective-permute-start.9) | collective-permute-done | bytes 8224 | tf_op jit(solution)/shard_map/ppermute | solution.py:237
  43.7 0.0 collective-permute-start.11
  43.7 0.0 collective-permute-done.10.refs_2_
  43.7 1.2 %collective-permute-done.11.refs_3_ = f32[8,256]{1,0:T(8,128)S(1)} collective-permute-done((f32[8,256]{1,0:T(8,128)S(1)}, f32[8,256]{1,0:T(8,128)S(1)}, u32[]{:S(2)}, u32[]{:S(2)}) %collective-permute-start.11) | collective-permute-done | bytes 8224 | tf_op jit(solution)/shard_map/ppermute | solution.py:240
  44.9 0.0 copy-done.7
  44.9 4.1 %grad.1 = (f32[1,256]{1,0:T(1,128)}, bf16[256,4096]{1,0:T(8,128)(2,1)S(1)}, bf16[256,512]{1,0:T(8,128)(2,1)S(1)}) custom-call(s32[1,8]{1,0:T(1,128)S(1)} %bitcast.10, f32[8,256]{1,0:T(8,128)S(1)} %get-tuple-element.19.refs_0_, f32[8,256]{1,0:T(8,128)S(1)} %collective-permute-done.9.refs_1_, f32[8,256]{1,0:T(8,128)S(1)} %collective-permute-done.10.refs_2_, ...), custom_call_target="tpu_custom_call" | custom-call | flops 2147483648 | tf_op jit(solution)/shard_map/grad/pallas_call | solution.py:297
  49.0 0.2 collective-permute-start.13
  49.2 1.3 %slice0_1.1 = bf16[256,512]{1,0:T(8,128)(2,1)S(1)} custom-call(bf16[256,4096]{1,0:T(8,128)(2,1)S(1)} %get-tuple-element.22.grads, bf16[2048,4096]{1,0:T(8,128)(2,1)S(1)} %copy-done.1), custom_call_target="tpu_custom_call" | custom-call | flops 1073741824 | tf_op jit(solution)/shard_map/slice0_1/pallas_call | solution.py:306
  50.5 0.4 collective-permute-start.12
  50.9 1.3 %slice1_0.1 = f32[256,512]{1,0:T(8,128)S(1)} custom-call(bf16[256,4096]{1,0:T(8,128)(2,1)S(1)} %get-tuple-element.22.grads, bf16[2048,4096]{1,0:T(8,128)(2,1)S(1)} %copy-done.1), custom_call_target="tpu_custom_call" | custom-call | flops 1073741824 | tf_op jit(solution)/shard_map/slice1_0/pallas_call | solution.py:306
  52.2 0.0 collective-permute-done.13
  52.2 0.1 add_convert_fusion
  52.3 1.6 %collective-permute-start.14 = (bf16[256,512]{1,0:T(8,128)(2,1)S(1)}, bf16[256,512]{1,0:T(8,128)(2,1)S(1)}, u32[]{:S(2)}, u32[]{:S(2)}) collective-permute-start(bf16[256,512]{1,0:T(8,128)(2,1)S(1)} %add_convert_fusion), channel_id=1, source_target_pairs={{0,2},{1,3},{2,0},{3,1},{4,6},{5,7},{6,4},{7,5},{8,10},{9,11},{10,... | collective-permute-start | bytes 786440 | tf_op jit(solution)/shard_map/ppermute | solution.py:237
  53.8 1.3 %slice0_0.1 = f32[256,512]{1,0:T(8,128)S(1)} custom-call(bf16[256,4096]{1,0:T(8,128)(2,1)S(1)} %get-tuple-element.22.grads, bf16[2048,4096]{1,0:T(8,128)(2,1)S(1)} %copy-done.1), custom_call_target="tpu_custom_call" | custom-call | flops 1073741824 | tf_op jit(solution)/shard_map/slice0_0/pallas_call | solution.py:306
  55.1 0.0 collective-permute-done.12
  55.1 5.6 %collective-permute-done.14 = bf16[256,512]{1,0:T(8,128)(2,1)S(1)} collective-permute-done((bf16[256,512]{1,0:T(8,128)(2,1)S(1)}, bf16[256,512]{1,0:T(8,128)(2,1)S(1)}, u32[]{:S(2)}, u32[]{:S(2)}) %collective-permute-start.14) | collective-permute-done | bytes 262176 | tf_op jit(solution)/shard_map/ppermute | solution.py:237
  60.7 0.8 %multiply_convert_fusion = bf16[256,512]{1,0:T(8,128)(2,1)} fusion(bf16[256,512]{1,0:T(8,128)(2,1)S(1)} %collective-permute-done.14, f32[256,512]{1,0:T(8,128)S(1)} %slice0_0.1, bf16[256,512]{1,0:T(8,128)(2,1)S(1)} %collective-permute-done.12), kind=kLoop, calls=%fused_computation | loop fusion | flops 786432 | bytes 1310720 | tf_op jit(solution)/shard_map/convert_element_type | solution.py:324
Async XLA Ops:
  0.6 17.0 %collective-permute-start.6 = (bf16[256,512]{1,0:T(8,128)(2,1)}, bf16[256,512]{1,0:T(8,128)(2,1)S(1)}, u32[]{:S(2)}, u32[]{:S(2)}) collective-permute-start(bf16[256,512]{1,0:T(8,128)(2,1)} %mine.1), channel_id=1, source_target_pairs={{0,2},{1,3},{2,0},{3,1},{4,6},{5,7},{6,4},{7,5},{8,10},{9,11},{10,... | collective-permute-start | bytes 786440 | tf_op jit(solution)/shard_map/ppermute | solution.py:237
  3.7 14.5 %collective-permute-start.8 = (bf16[256,512]{1,0:T(8,128)(2,1)}, bf16[256,512]{1,0:T(8,128)(2,1)S(1)}, u32[]{:S(2)}, u32[]{:S(2)}) collective-permute-start(bf16[256,512]{1,0:T(8,128)(2,1)} %mine.1), channel_id=1, source_target_pairs={{0,1},{1,0},{2,3},{3,2},{4,5},{5,4},{6,7},{7,6},{8,9},{9,8},{10,11... | collective-permute-start | bytes 786440 | tf_op jit(solution)/shard_map/ppermute | solution.py:240
  3.7 1.0 %copy-start.3 = (bf16[256,512]{1,0:T(8,128)(2,1)S(1)}, bf16[256,512]{1,0:T(8,128)(2,1)}, u32[]{:S(2)}) copy-start(bf16[256,512]{1,0:T(8,128)(2,1)} %rows_ref.1) | copy-start | bytes 786436
  4.6 0.7 %copy-start.6 = (s32[256]{0:T(256)S(1)}, s32[256]{0:T(256)}, u32[]{:S(2)}) copy-start(s32[256]{0:T(256)} %param.12) | copy-start | bytes 3076
  5.7 7.9 %collective-permute-start = (bf16[72,512]{1,0:T(8,128)(2,1)S(1)}, bf16[72,512]{1,0:T(8,128)(2,1)S(1)}, u32[]{:S(2)}, u32[]{:S(2)}) collective-permute-start(bf16[72,512]{1,0:T(8,128)(2,1)S(1)} %get-tuple-element.14), channel_id=1, source_target_pairs={{0,4},{4,8},{8,12},{12,16},{16,20},{20,24},{24,28},{28,0},{1,5},{5... | collective-permute-start | bytes 221192 | tf_op jit(solution)/shard_map/ppermute | solution.py:234
  7.3 8.5 %collective-permute-start.1 = (bf16[72,512]{1,0:T(8,128)(2,1)S(1)}, bf16[72,512]{1,0:T(8,128)(2,1)S(1)}, u32[]{:S(2)}, u32[]{:S(2)}) collective-permute-start(bf16[72,512]{1,0:T(8,128)(2,1)S(1)} %get-tuple-element.15), channel_id=1, source_target_pairs={{0,16},{4,20},{8,24},{12,28},{16,0},{20,4},{24,8},{28,12},{1,17},{... | collective-permute-start | bytes 221192 | tf_op jit(solution)/shard_map/ppermute | solution.py:234
  9.9 6.7 %collective-permute-start.2 = (bf16[72,512]{1,0:T(8,128)(2,1)S(1)}, bf16[72,512]{1,0:T(8,128)(2,1)S(1)}, u32[]{:S(2)}, u32[]{:S(2)}) collective-permute-start(bf16[72,512]{1,0:T(8,128)(2,1)S(1)} %get-tuple-element.16), channel_id=1, source_target_pairs={{0,20},{4,24},{8,28},{12,0},{16,4},{20,8},{24,12},{28,16},{1,21},{... | collective-permute-start | bytes 221192 | tf_op jit(solution)/shard_map/ppermute | solution.py:234
  17.0 10.2 %collective-permute-start.3 = (bf16[256,512]{1,0:T(8,128)(2,1)S(1)}, bf16[256,512]{1,0:T(8,128)(2,1)S(1)}, u32[]{:S(2)}, u32[]{:S(2)}) collective-permute-start(bf16[256,512]{1,0:T(8,128)(2,1)S(1)} %unpack.1.mine), channel_id=1, source_target_pairs={{0,2},{1,3},{2,0},{3,1},{4,6},{5,7},{6,4},{7,5},{8,10},{9,11},{10,... | collective-permute-start | bytes 786440 | tf_op jit(solution)/shard_map/ppermute | solution.py:237
  17.6 9.7 %collective-permute-start.5 = (bf16[256,512]{1,0:T(8,128)(2,1)S(1)}, bf16[256,512]{1,0:T(8,128)(2,1)S(1)}, u32[]{:S(2)}, u32[]{:S(2)}) collective-permute-start(bf16[256,512]{1,0:T(8,128)(2,1)S(1)} %unpack.1.mine), channel_id=1, source_target_pairs={{0,1},{1,0},{2,3},{3,2},{4,5},{5,4},{6,7},{7,6},{8,9},{9,8},{10,11... | collective-permute-start | bytes 786440 | tf_op jit(solution)/shard_map/ppermute | solution.py:240
  17.7 15.4 %collective-permute-start.7 = (bf16[256,512]{1,0:T(8,128)(2,1)S(1)}, bf16[256,512]{1,0:T(8,128)(2,1)S(1)}, u32[]{:S(2)}, u32[]{:S(2)}) collective-permute-start(bf16[256,512]{1,0:T(8,128)(2,1)S(1)} %collective-permute-done.6.mine), channel_id=1, source_target_pairs={{0,1},{1,0},{2,3},{3,2},{4,5},{5,4},{6,7},{7,6},{8,9},{9,8},{10,11... | collective-permute-start | bytes 786440 | tf_op jit(solution)/shard_map/ppermute | solution.py:240
  18.2 5.8 %copy-start = (bf16[2048,4096]{1,0:T(8,128)(2,1)S(1)}, bf16[2048,4096]{1,0:T(8,128)(2,1)}, u32[]{:S(2)}) copy-start(bf16[2048,4096]{1,0:T(8,128)(2,1)} %head.13) | copy-start | bytes 50331652
  23.9 0.9 %copy-start.2 = (bf16[256,512]{1,0:T(8,128)(2,1)S(1)}, bf16[256,512]{1,0:T(8,128)(2,1)}, u32[]{:S(2)}) copy-start(bf16[256,512]{1,0:T(8,128)(2,1)} %mine.1) | copy-start | bytes 786436
  24.9 5.8 %copy-start.1 = (bf16[2048,4096]{1,0:T(8,128)(2,1)S(1)}, bf16[2048,4096]{1,0:T(8,128)(2,1)}, u32[]{:S(2)}) copy-start(bf16[2048,4096]{1,0:T(8,128)(2,1)} %head.13) | copy-start | bytes 50331652
  27.3 5.8 %copy-start.4 = (s32[4096]{0:T(1024)S(1)}, s32[4096]{0:T(1024)}, u32[]{:S(2)}) copy-start(s32[4096]{0:T(1024)} %param.10) | copy-start | bytes 49156
  27.3 5.8 %copy-start.5 = (s32[256]{0:T(256)S(1)}, s32[256]{0:T(256)}, u32[]{:S(2)}) copy-start(s32[256]{0:T(256)} %param.11) | copy-start | bytes 3076
  27.3 9.4 %collective-permute-start.4 = (bf16[256,512]{1,0:T(8,128)(2,1)S(1)}, bf16[256,512]{1,0:T(8,128)(2,1)S(1)}, u32[]{:S(2)}, u32[]{:S(2)}) collective-permute-start(bf16[256,512]{1,0:T(8,128)(2,1)S(1)} %collective-permute-done.3.mine), channel_id=1, source_target_pairs={{0,1},{1,0},{2,3},{3,2},{4,5},{5,4},{6,7},{7,6},{8,9},{9,8},{10,11... | collective-permute-start | bytes 786440 | tf_op jit(solution)/shard_map/ppermute | solution.py:240
  36.7 8.2 %copy-start.7 = (s32[8]{0:T(128)S(1)}, s32[8]{0:T(128)}, u32[]{:S(2)}) copy-start(s32[8]{0:T(128)} %param.13) | copy-start | bytes 100
  40.0 3.7 %collective-permute-start.9 = (f32[8,256]{1,0:T(8,128)S(1)}, f32[8,256]{1,0:T(8,128)S(1)}, u32[]{:S(2)}, u32[]{:S(2)}) collective-permute-start(f32[8,256]{1,0:T(8,128)S(1)} %get-tuple-element.19.refs_0_), channel_id=1, source_target_pairs={{0,2},{1,3},{2,0},{3,1},{4,6},{5,7},{6,4},{7,5},{8,10},{9,11},{10,... | collective-permute-start | bytes 24584 | tf_op jit(solution)/shard_map/ppermute | solution.py:237
  41.6 2.2 %collective-permute-start.10 = (f32[8,256]{1,0:T(8,128)S(1)}, f32[8,256]{1,0:T(8,128)S(1)}, u32[]{:S(2)}, u32[]{:S(2)}) collective-permute-start(f32[8,256]{1,0:T(8,128)S(1)} %get-tuple-element.19.refs_0_), channel_id=1, source_target_pairs={{0,1},{1,0},{2,3},{3,2},{4,5},{5,4},{6,7},{7,6},{8,9},{9,8},{10,11... | collective-permute-start | bytes 24584 | tf_op jit(solution)/shard_map/ppermute | solution.py:240
  43.7 1.2 %collective-permute-start.11 = (f32[8,256]{1,0:T(8,128)S(1)}, f32[8,256]{1,0:T(8,128)S(1)}, u32[]{:S(2)}, u32[]{:S(2)}) collective-permute-start(f32[8,256]{1,0:T(8,128)S(1)} %collective-permute-done.9.refs_1_), channel_id=1, source_target_pairs={{0,1},{1,0},{2,3},{3,2},{4,5},{5,4},{6,7},{7,6},{8,9},{9,8},{10,11... | collective-permute-start | bytes 24584 | tf_op jit(solution)/shard_map/ppermute | solution.py:240
  49.0 3.1 %collective-permute-start.13 = (bf16[256,512]{1,0:T(8,128)(2,1)S(1)}, bf16[256,512]{1,0:T(8,128)(2,1)S(1)}, u32[]{:S(2)}, u32[]{:S(2)}) collective-permute-start(bf16[256,512]{1,0:T(8,128)(2,1)S(1)} %get-tuple-element.23), channel_id=1, source_target_pairs={{0,1},{1,0},{2,3},{3,2},{4,5},{5,4},{6,7},{7,6},{8,9},{9,8},{10,11... | collective-permute-start | bytes 786440 | tf_op jit(solution)/shard_map/ppermute | solution.py:240
  50.5 4.6 %collective-permute-start.12 = (bf16[256,512]{1,0:T(8,128)(2,1)S(1)}, bf16[256,512]{1,0:T(8,128)(2,1)S(1)}, u32[]{:S(2)}, u32[]{:S(2)}) collective-permute-start(bf16[256,512]{1,0:T(8,128)(2,1)S(1)} %slice0_1.1), channel_id=1, source_target_pairs={{0,1},{1,0},{2,3},{3,2},{4,5},{5,4},{6,7},{7,6},{8,9},{9,8},{10,11... | collective-permute-start | bytes 786440 | tf_op jit(solution)/shard_map/ppermute | solution.py:240
  52.3 8.4 %collective-permute-start.14 = (bf16[256,512]{1,0:T(8,128)(2,1)S(1)}, bf16[256,512]{1,0:T(8,128)(2,1)S(1)}, u32[]{:S(2)}, u32[]{:S(2)}) collective-permute-start(bf16[256,512]{1,0:T(8,128)(2,1)S(1)} %add_convert_fusion), channel_id=1, source_target_pairs={{0,2},{1,3},{2,0},{3,1},{4,6},{5,7},{6,4},{7,5},{8,10},{9,11},{10,... | collective-permute-start | bytes 786440 | tf_op jit(solution)/shard_map/ppermute | solution.py:237
